TPU v7x, 32 devices: a whole 2x2x4 slice. The times are simulated.
32 devices in a mesh: ctx: 8 (over z, y), head: 4 (over x, core).
Axes of the slice: x: 2, y: 2, z: 4, core: 2. Of those that a mesh axis runs over, the one named last changes fastest.
Arguments:
- queries: bfloat16 [8192, 1024], P('ctx', 'head'), parts along dimension 1, may hold values from -15 to 15
- key_rows: bfloat16 [8192, 512], P('ctx', 'head'), parts along dimension 1, may hold values from -6 to 6
- value_rows: bfloat16 [8192, 512], P('ctx', 'head'), parts along dimension 1, may hold values from -16 to 16
- block_order: int32 [8], replicated, may hold values from 0 to 7, each once
Outputs:
- attended: bfloat16 [8192, 1024], P('ctx', 'head'), parts along dimension 1
There are 4 independent parts, one for each index of `head`. A program takes and returns all parts, laid end to end along the dimension named above; an argument that names none is the same for every part. Nothing has to cross between parts.
Inputs may be any that keep to these rules, and one draw needn't show every extreme that they name: `block_order`: each block number appears once.
All inputs are finite; a program needn't handle non-finite values.
Results may differ from a plain program's by a relative error of at most 0.0033.
Values may be sent and summed in bfloat16 or wider, within the bound.
A program may use at most 128 MiB of HBM per device.

v0:
```python
import jax
import jax.numpy as jnp
from jax import lax
from jax.sharding import PartitionSpec as P

HD = 128
QH = 2


score_scale = 168.0 ** (-0.5)


def shifted(array, axis, by):
    count = lax.axis_size(axis)
    return lax.ppermute(array, axis, [(i, (i + by) % count) for i in range(count)])


def score_tile(query_block, key_block, causal):
    query_heads = query_block.reshape(query_block.shape[0], QH, HD)
    scores = (
        jnp.einsum("qhd,kd->hqk", query_heads, key_block, preferred_element_type=jnp.float32)
        * score_scale
    )
    if causal:
        length = scores.shape[1]
        row_ids = lax.broadcasted_iota(jnp.int32, (length, length), 0)
        column_ids = lax.broadcasted_iota(jnp.int32, (length, length), 1)
        scores = jnp.where((column_ids <= row_ids)[None], scores, -jnp.inf)
    return scores


def fresh_partial(scores, value_block):
    row_max = jnp.max(scores, axis=2)
    weights = jnp.exp(scores - row_max[:, :, None])
    row_total = jnp.sum(weights, axis=2)
    summed = jnp.einsum(
        "hqk,kd->hqd", weights.astype(jnp.bfloat16), value_block, preferred_element_type=jnp.float32
    )
    return (summed, row_max, row_total)


def combine_partial(carried, incoming):
    sum_first, max_first, total_first = carried
    sum_second, max_second, total_second = incoming
    new_max = jnp.maximum(max_first, max_second)
    scale_first = jnp.exp(max_first - new_max)
    scale_second = jnp.exp(max_second - new_max)
    new_sum = sum_first * scale_first[:, :, None] + sum_second * scale_second[:, :, None]
    return (new_sum, new_max, total_first * scale_first + total_second * scale_second)


def absorb(carried, scores, value_block):
    return combine_partial(carried, fresh_partial(scores, value_block))


def body(queries, key_rows, value_rows, block_order):
    devices = lax.axis_size("ctx")
    my_index = lax.axis_index("ctx")
    my_block = block_order[my_index]
    carried = fresh_partial(score_tile(queries, key_rows, True), value_rows)

    def cycle_step(offset, loop_carry):
        moving_keys, moving_values, running = loop_carry
        moving_keys, moving_values = shifted((moving_keys, moving_values), "ctx", 1)
        source = (my_index - offset) % devices
        running = lax.cond(
            block_order[source] < my_block,
            lambda: absorb(running, score_tile(queries, moving_keys, False), moving_values),
            lambda: running,
        )
        return (moving_keys, moving_values, running)

    spent_keys, spent_values, carried = lax.fori_loop(
        1, devices, cycle_step, (key_rows, value_rows, carried)
    )
    final_sum, final_max, final_total = carried
    attended = final_sum / final_total[:, :, None]
    return attended.transpose(1, 0, 2).reshape(queries.shape[0], QH * HD).astype(jnp.bfloat16)


def solution(mesh):
    in_specs = (P("ctx", "head"), P("ctx", "head"), P("ctx", "head"), P())
    out_specs = P("ctx", "head")
    return jax.shard_map(body, mesh=mesh, in_specs=in_specs, out_specs=out_specs, check_vma=False)
```

profile of v0, /device:TPU:0, one launch (start us, length us, event | category | flops | bytes accessed | tf_op | source)
XLA Modules:
  0.0 133.7 jit_solution(6946959007157523607)
XLA Ops:
  2.2 2.8 %fusion.21 = (f32[2,1024]{1,0:T(2,128)S(1)}, f32[1024,1024,2]{1,0,2:T(8,128)S(1)}) fusion(pred[1024,1024]{0,1:T(8,128)(4,1)S(1)} %iota_compare_fusion, bf16[1024,128]{1,0:T(8,128)(2,1)S(1)} %copy.54, bf16[1024,256]{1,0:T(8,128)(2,1)} %param.8), kind=kOutput, calls=%fused_computation.23 | convolution fusion | flops 543160320 | bytes 10231808 | tf_op jit(solution)/shard_map/qhd,kd->hqk/dot_general | solution.py:21
  5.0 2.5 %fusion.22 = f32[2,1024,128]{2,1,0:T(8,128)S(1)} fusion(f32[1024,1024,2]{1,0,2:T(8,128)S(1)} %get-tuple-element.320, f32[2,1024]{1,0:T(2,128)S(1)} %get-tuple-element.398, pred[1024,1024]{0,1:T(8,128)(4,1)S(1)} %iota_compare_fusion, bf16[1024,128]{1,0:T(8,128)(2,1)S(1)} %copy.55), kind=kOutput, calls=%fused_computation.25 | convolution fusion | flops 545259520 | bytes 10756096 | tf_op jit(solution)/shard_map/hqk,kd->hqd/dot_general | solution.py:36
  7.6 2.0 %fusion.19 = f32[2,1024]{1,0:T(2,128)S(1)} fusion(f32[1024,1024,2]{1,0,2:T(8,128)S(1)} %get-tuple-element.320, f32[2,1024]{1,0:T(2,128)S(1)} %get-tuple-element.398, pred[1024,1024]{0,1:T(8,128)(4,1)S(1)} %iota_compare_fusion), kind=kLoop, calls=%fused_computation.21 | loop fusion | flops 8386560 | bytes 9453568 | tf_op jit(solution)/shard_map/reduce_sum | solution.py:35
  10.2 122.4 %while.23 = (s32[]{:T(128)}, bf16[1024,128]{1,0:T(8,128)(2,1)S(1)}, bf16[1024,128]{1,0:T(8,128)(2,1)S(1)}, f32[2,1024,128]{2,1,0:T(8,128)S(1)}, f32[2,1024]{1,0:...) while((s32[]{:T(128)}, bf16[1024,128]{1,0:T(8,128)(2,1)S(1)}, ...), condition=%wide.region_7.8_spmd, body=%wide.region_2.7_spmd.sunk | while | flops 1091313664 | bytes 31572464 | solution.py:73
  10.2 3.0 %collective-permute-start = (bf16[1024,128]{1,0:T(8,128)(2,1)S(1)}, bf16[1024,128]{1,0:T(8,128)(2,1)S(1)}, u32[]{:S(2)}, u32[]{:S(2)}) collective-permute-start(bf16[1024,128]{1,0:T(8,128)(2,1)S(1)} %get-tuple-element.409), channel_id=1, source_target_pairs={{0,4},{4,8},{8,12},{12,16},{16,20},{20,24},{24,28},{28,0},{1,5},{5... | collective-permute-start | bytes 786440 | tf_op jit(solution)/shard_map/while/body/eval_jaxpr/ppermute | solution.py:15
  13.2 1.5 %collective-permute-start.1 = (bf16[1024,128]{1,0:T(8,128)(2,1)S(1)}, bf16[1024,128]{1,0:T(8,128)(2,1)S(1)}, u32[]{:S(2)}, u32[]{:S(2)}) collective-permute-start(bf16[1024,128]{1,0:T(8,128)(2,1)S(1)} %get-tuple-element.410), channel_id=1, source_target_pairs={{0,4},{4,8},{8,12},{12,16},{16,20},{20,24},{24,28},{28,0},{1,5},{5... | collective-permute-start | bytes 786440 | tf_op jit(solution)/shard_map/while/body/eval_jaxpr/ppermute | solution.py:15
  16.5 6.9 %collective-permute-done = bf16[1024,128]{1,0:T(8,128)(2,1)S(1)} collective-permute-done((bf16[1024,128]{1,0:T(8,128)(2,1)S(1)}, bf16[1024,128]{1,0:T(8,128)(2,1)S(1)}, u32[]{:S(2)}, u32[]{:S(2)}) %collective-permute-start) | collective-permute-done | bytes 262176 | tf_op jit(solution)/shard_map/while/body/eval_jaxpr/ppermute | solution.py:15
  23.4 4.8 %collective-permute-done.1 = bf16[1024,128]{1,0:T(8,128)(2,1)S(1)} collective-permute-done((bf16[1024,128]{1,0:T(8,128)(2,1)S(1)}, bf16[1024,128]{1,0:T(8,128)(2,1)S(1)}, u32[]{:S(2)}, u32[]{:S(2)}) %collective-permute-start.1) | collective-permute-done | bytes 262176 | tf_op jit(solution)/shard_map/while/body/eval_jaxpr/ppermute | solution.py:15
  28.2 3.6 %collective-permute-start = (bf16[1024,128]{1,0:T(8,128)(2,1)S(1)}, bf16[1024,128]{1,0:T(8,128)(2,1)S(1)}, u32[]{:S(2)}, u32[]{:S(2)}) collective-permute-start(bf16[1024,128]{1,0:T(8,128)(2,1)S(1)} %get-tuple-element.409), channel_id=1, source_target_pairs={{0,4},{4,8},{8,12},{12,16},{16,20},{20,24},{24,28},{28,0},{1,5},{5... | collective-permute-start | bytes 786440 | tf_op jit(solution)/shard_map/while/body/eval_jaxpr/ppermute | solution.py:15
  33.7 8.3 %collective-permute-done = bf16[1024,128]{1,0:T(8,128)(2,1)S(1)} collective-permute-done((bf16[1024,128]{1,0:T(8,128)(2,1)S(1)}, bf16[1024,128]{1,0:T(8,128)(2,1)S(1)}, u32[]{:S(2)}, u32[]{:S(2)}) %collective-permute-start) | collective-permute-done | bytes 262176 | tf_op jit(solution)/shard_map/while/body/eval_jaxpr/ppermute | solution.py:15
  42.0 3.9 %collective-permute-done.1 = bf16[1024,128]{1,0:T(8,128)(2,1)S(1)} collective-permute-done((bf16[1024,128]{1,0:T(8,128)(2,1)S(1)}, bf16[1024,128]{1,0:T(8,128)(2,1)S(1)}, u32[]{:S(2)}, u32[]{:S(2)}) %collective-permute-start.1) | collective-permute-done | bytes 262176 | tf_op jit(solution)/shard_map/while/body/eval_jaxpr/ppermute | solution.py:15
  46.0 4.9 %conditional.2 = ((f32[2,1024,128]{2,1,0:T(8,128)S(1)}, f32[2,1024]{1,0:T(2,128)S(1)}, f32[2,1024]{1,0:T(2,128)S(1)})) conditional(s32[]{:T(128)} %convert_element_type.42, (f32[2,1024,128]{2,1,0:T(8,128)S(1)}, f32[2,1024]{1,0:T(2,128)S(1)}, f32[2,1024]{1,0:T(2,128)S(1)}) %tuple.50, (bf16[1024,256]{1,0:T(8,128)(2,1)S(1)}, ...), branch_computations={%region_3.3_spmd, %region_4.6_spmd} | conditional | flops 1091313664 | bytes 28426272 | solution.py:66
  47.2 1.4 %fusion.1 = f32[2,1024]{1,0:T(2,128)S(1)} fusion(f32[1024,1024,2]{1,0,2:T(8,128)S(1)} %get-tuple-element.318, f32[2,1024]{1,0:T(2,128)S(1)} %get-tuple-element.317), kind=kLoop, calls=%fused_computation.3 | loop fusion | flops 6289408 | bytes 8404992 | tf_op jit(solution)/shard_map/while/body/eval_jaxpr/cond/branch_1_fun/reduce_sum | solution.py:35
  48.6 2.2 %fusion.10 = f32[2,1024,128]{2,1,0:T(8,128)S(1)} fusion(f32[1024,1024,2]{1,0,2:T(8,128)S(1)} %get-tuple-element.318, f32[2,1024]{1,0:T(2,128)S(1)} %get-tuple-element.317, f32[2,1024,128]{2,1,0:T(8,128)S(1)} %get-tuple-element.269, f32[2,1024]{1,0:T(2,128)S(1)} %get-tuple-element.315, f32[2,1024]{1,0:T(2,128)S(1)} %get-tuple-element.314, ...), kind=kOutput, calls=%fused_computation.9 | convolution fusion | flops 543948800 | bytes 10772480 | tf_op jit(solution)/shard_map/while/body/eval_jaxpr/cond/branch_1_fun/hqk,kd->hqd/dot_general | solution.py:36
  52.9 10.0 %collective-permute-done = bf16[1024,128]{1,0:T(8,128)(2,1)S(1)} collective-permute-done((bf16[1024,128]{1,0:T(8,128)(2,1)S(1)}, bf16[1024,128]{1,0:T(8,128)(2,1)S(1)}, u32[]{:S(2)}, u32[]{:S(2)}) %collective-permute-start) | collective-permute-done | bytes 262176 | tf_op jit(solution)/shard_map/while/body/eval_jaxpr/ppermute | solution.py:15
  62.8 3.0 %collective-permute-done.1 = bf16[1024,128]{1,0:T(8,128)(2,1)S(1)} collective-permute-done((bf16[1024,128]{1,0:T(8,128)(2,1)S(1)}, bf16[1024,128]{1,0:T(8,128)(2,1)S(1)}, u32[]{:S(2)}, u32[]{:S(2)}) %collective-permute-start.1) | collective-permute-done | bytes 262176 | tf_op jit(solution)/shard_map/while/body/eval_jaxpr/ppermute | solution.py:15
  66.0 2.5 %collective-permute-start = (bf16[1024,128]{1,0:T(8,128)(2,1)S(1)}, bf16[1024,128]{1,0:T(8,128)(2,1)S(1)}, u32[]{:S(2)}, u32[]{:S(2)}) collective-permute-start(bf16[1024,128]{1,0:T(8,128)(2,1)S(1)} %get-tuple-element.409), channel_id=1, source_target_pairs={{0,4},{4,8},{8,12},{12,16},{16,20},{20,24},{24,28},{28,0},{1,5},{5... | collective-permute-start | bytes 786440 | tf_op jit(solution)/shard_map/while/body/eval_jaxpr/ppermute | solution.py:15
  70.4 6.9 %collective-permute-done = bf16[1024,128]{1,0:T(8,128)(2,1)S(1)} collective-permute-done((bf16[1024,128]{1,0:T(8,128)(2,1)S(1)}, bf16[1024,128]{1,0:T(8,128)(2,1)S(1)}, u32[]{:S(2)}, u32[]{:S(2)}) %collective-permute-start) | collective-permute-done | bytes 262176 | tf_op jit(solution)/shard_map/while/body/eval_jaxpr/ppermute | solution.py:15
  77.3 2.8 %collective-permute-done.1 = bf16[1024,128]{1,0:T(8,128)(2,1)S(1)} collective-permute-done((bf16[1024,128]{1,0:T(8,128)(2,1)S(1)}, bf16[1024,128]{1,0:T(8,128)(2,1)S(1)}, u32[]{:S(2)}, u32[]{:S(2)}) %collective-permute-start.1) | collective-permute-done | bytes 262176 | tf_op jit(solution)/shard_map/while/body/eval_jaxpr/ppermute | solution.py:15
  80.1 4.9 %conditional.2 = ((f32[2,1024,128]{2,1,0:T(8,128)S(1)}, f32[2,1024]{1,0:T(2,128)S(1)}, f32[2,1024]{1,0:T(2,128)S(1)})) conditional(s32[]{:T(128)} %convert_element_type.42, (f32[2,1024,128]{2,1,0:T(8,128)S(1)}, f32[2,1024]{1,0:T(2,128)S(1)}, f32[2,1024]{1,0:T(2,128)S(1)}) %tuple.50, (bf16[1024,256]{1,0:T(8,128)(2,1)S(1)}, ...), branch_computations={%region_3.3_spmd, %region_4.6_spmd} | conditional | flops 1091313664 | bytes 28426272 | solution.py:66
  81.3 1.4 %fusion.1 = f32[2,1024]{1,0:T(2,128)S(1)} fusion(f32[1024,1024,2]{1,0,2:T(8,128)S(1)} %get-tuple-element.318, f32[2,1024]{1,0:T(2,128)S(1)} %get-tuple-element.317), kind=kLoop, calls=%fused_computation.3 | loop fusion | flops 6289408 | bytes 8404992 | tf_op jit(solution)/shard_map/while/body/eval_jaxpr/cond/branch_1_fun/reduce_sum | solution.py:35
  82.8 2.2 %fusion.10 = f32[2,1024,128]{2,1,0:T(8,128)S(1)} fusion(f32[1024,1024,2]{1,0,2:T(8,128)S(1)} %get-tuple-element.318, f32[2,1024]{1,0:T(2,128)S(1)} %get-tuple-element.317, f32[2,1024,128]{2,1,0:T(8,128)S(1)} %get-tuple-element.269, f32[2,1024]{1,0:T(2,128)S(1)} %get-tuple-element.315, f32[2,1024]{1,0:T(2,128)S(1)} %get-tuple-element.314, ...), kind=kOutput, calls=%fused_computation.9 | convolution fusion | flops 543948800 | bytes 10772480 | tf_op jit(solution)/shard_map/while/body/eval_jaxpr/cond/branch_1_fun/hqk,kd->hqd/dot_general | solution.py:36
  87.0 8.5 %collective-permute-done = bf16[1024,128]{1,0:T(8,128)(2,1)S(1)} collective-permute-done((bf16[1024,128]{1,0:T(8,128)(2,1)S(1)}, bf16[1024,128]{1,0:T(8,128)(2,1)S(1)}, u32[]{:S(2)}, u32[]{:S(2)}) %collective-permute-start) | collective-permute-done | bytes 262176 | tf_op jit(solution)/shard_map/while/body/eval_jaxpr/ppermute | solution.py:15
  95.5 2.8 %collective-permute-done.1 = bf16[1024,128]{1,0:T(8,128)(2,1)S(1)} collective-permute-done((bf16[1024,128]{1,0:T(8,128)(2,1)S(1)}, bf16[1024,128]{1,0:T(8,128)(2,1)S(1)}, u32[]{:S(2)}, u32[]{:S(2)}) %collective-permute-start.1) | collective-permute-done | bytes 262176 | tf_op jit(solution)/shard_map/while/body/eval_jaxpr/ppermute | solution.py:15
  98.3 4.9 %conditional.2 = ((f32[2,1024,128]{2,1,0:T(8,128)S(1)}, f32[2,1024]{1,0:T(2,128)S(1)}, f32[2,1024]{1,0:T(2,128)S(1)})) conditional(s32[]{:T(128)} %convert_element_type.42, (f32[2,1024,128]{2,1,0:T(8,128)S(1)}, f32[2,1024]{1,0:T(2,128)S(1)}, f32[2,1024]{1,0:T(2,128)S(1)}) %tuple.50, (bf16[1024,256]{1,0:T(8,128)(2,1)S(1)}, ...), branch_computations={%region_3.3_spmd, %region_4.6_spmd} | conditional | flops 1091313664 | bytes 28426272 | solution.py:66
  101.0 2.2 %fusion.10 = f32[2,1024,128]{2,1,0:T(8,128)S(1)} fusion(f32[1024,1024,2]{1,0,2:T(8,128)S(1)} %get-tuple-element.318, f32[2,1024]{1,0:T(2,128)S(1)} %get-tuple-element.317, f32[2,1024,128]{2,1,0:T(8,128)S(1)} %get-tuple-element.269, f32[2,1024]{1,0:T(2,128)S(1)} %get-tuple-element.315, f32[2,1024]{1,0:T(2,128)S(1)} %get-tuple-element.314, ...), kind=kOutput, calls=%fused_computation.9 | convolution fusion | flops 543948800 | bytes 10772480 | tf_op jit(solution)/shard_map/while/body/eval_jaxpr/cond/branch_1_fun/hqk,kd->hqd/dot_general | solution.py:36
  105.2 7.6 %collective-permute-done = bf16[1024,128]{1,0:T(8,128)(2,1)S(1)} collective-permute-done((bf16[1024,128]{1,0:T(8,128)(2,1)S(1)}, bf16[1024,128]{1,0:T(8,128)(2,1)S(1)}, u32[]{:S(2)}, u32[]{:S(2)}) %collective-permute-start) | collective-permute-done | bytes 262176 | tf_op jit(solution)/shard_map/while/body/eval_jaxpr/ppermute | solution.py:15
  112.9 2.8 %collective-permute-done.1 = bf16[1024,128]{1,0:T(8,128)(2,1)S(1)} collective-permute-done((bf16[1024,128]{1,0:T(8,128)(2,1)S(1)}, bf16[1024,128]{1,0:T(8,128)(2,1)S(1)}, u32[]{:S(2)}, u32[]{:S(2)}) %collective-permute-start.1) | collective-permute-done | bytes 262176 | tf_op jit(solution)/shard_map/while/body/eval_jaxpr/ppermute | solution.py:15
  115.7 4.9 %conditional.2 = ((f32[2,1024,128]{2,1,0:T(8,128)S(1)}, f32[2,1024]{1,0:T(2,128)S(1)}, f32[2,1024]{1,0:T(2,128)S(1)})) conditional(s32[]{:T(128)} %convert_element_type.42, (f32[2,1024,128]{2,1,0:T(8,128)S(1)}, f32[2,1024]{1,0:T(2,128)S(1)}, f32[2,1024]{1,0:T(2,128)S(1)}) %tuple.50, (bf16[1024,256]{1,0:T(8,128)(2,1)S(1)}, ...), branch_computations={%region_3.3_spmd, %region_4.6_spmd} | conditional | flops 1091313664 | bytes 28426272 | solution.py:66
  118.3 2.2 %fusion.10 = f32[2,1024,128]{2,1,0:T(8,128)S(1)} fusion(f32[1024,1024,2]{1,0,2:T(8,128)S(1)} %get-tuple-element.318, f32[2,1024]{1,0:T(2,128)S(1)} %get-tuple-element.317, f32[2,1024,128]{2,1,0:T(8,128)S(1)} %get-tuple-element.269, f32[2,1024]{1,0:T(2,128)S(1)} %get-tuple-element.315, f32[2,1024]{1,0:T(2,128)S(1)} %get-tuple-element.314, ...), kind=kOutput, calls=%fused_computation.9 | convolution fusion | flops 543948800 | bytes 10772480 | tf_op jit(solution)/shard_map/while/body/eval_jaxpr/cond/branch_1_fun/hqk,kd->hqd/dot_general | solution.py:36
  122.6 7.2 %collective-permute-done = bf16[1024,128]{1,0:T(8,128)(2,1)S(1)} collective-permute-done((bf16[1024,128]{1,0:T(8,128)(2,1)S(1)}, bf16[1024,128]{1,0:T(8,128)(2,1)S(1)}, u32[]{:S(2)}, u32[]{:S(2)}) %collective-permute-start) | collective-permute-done | bytes 262176 | tf_op jit(solution)/shard_map/while/body/eval_jaxpr/ppermute | solution.py:15
  129.7 2.8 %collective-permute-done.1 = bf16[1024,128]{1,0:T(8,128)(2,1)S(1)} collective-permute-done((bf16[1024,128]{1,0:T(8,128)(2,1)S(1)}, bf16[1024,128]{1,0:T(8,128)(2,1)S(1)}, u32[]{:S(2)}, u32[]{:S(2)}) %collective-permute-start.1) | collective-permute-done | bytes 262176 | tf_op jit(solution)/shard_map/while/body/eval_jaxpr/ppermute | solution.py:15
  (53 shorter events, 17.1 us)
Async XLA Ops:
  7.6 2.0 %copy-start.1 = (s32[8]{0:T(128)S(1)}, s32[8]{0:T(128)}, u32[]{:S(2)}) copy-start(s32[8]{0:T(128)} %param.11) | copy-start | bytes 100
  7.6 2.6 %copy-start = (bf16[1024,256]{1,0:T(8,128)(2,1)S(1)}, bf16[1024,256]{1,0:T(8,128)(2,1)}, u32[]{:S(2)}) copy-start(bf16[1024,256]{1,0:T(8,128)(2,1)} %param.8) | copy-start | bytes 1572868
  10.2 13.2 %collective-permute-start = (bf16[1024,128]{1,0:T(8,128)(2,1)S(1)}, bf16[1024,128]{1,0:T(8,128)(2,1)S(1)}, u32[]{:S(2)}, u32[]{:S(2)}) collective-permute-start(bf16[1024,128]{1,0:T(8,128)(2,1)S(1)} %get-tuple-element.409), channel_id=1, source_target_pairs={{0,4},{4,8},{8,12},{12,16},{16,20},{20,24},{24,28},{28,0},{1,5},{5... | collective-permute-start | bytes 786440 | tf_op jit(solution)/shard_map/while/body/eval_jaxpr/ppermute | solution.py:15
  13.2 15.0 %collective-permute-start.1 = (bf16[1024,128]{1,0:T(8,128)(2,1)S(1)}, bf16[1024,128]{1,0:T(8,128)(2,1)S(1)}, u32[]{:S(2)}, u32[]{:S(2)}) collective-permute-start(bf16[1024,128]{1,0:T(8,128)(2,1)S(1)} %get-tuple-element.410), channel_id=1, source_target_pairs={{0,4},{4,8},{8,12},{12,16},{16,20},{20,24},{24,28},{28,0},{1,5},{5... | collective-permute-start | bytes 786440 | tf_op jit(solution)/shard_map/while/body/eval_jaxpr/ppermute | solution.py:15
  28.2 13.8 %collective-permute-start = (bf16[1024,128]{1,0:T(8,128)(2,1)S(1)}, bf16[1024,128]{1,0:T(8,128)(2,1)S(1)}, u32[]{:S(2)}, u32[]{:S(2)}) collective-permute-start(bf16[1024,128]{1,0:T(8,128)(2,1)S(1)} %get-tuple-element.409), channel_id=1, source_target_pairs={{0,4},{4,8},{8,12},{12,16},{16,20},{20,24},{24,28},{28,0},{1,5},{5... | collective-permute-start | bytes 786440 | tf_op jit(solution)/shard_map/while/body/eval_jaxpr/ppermute | solution.py:15
  31.8 14.1 %collective-permute-start.1 = (bf16[1024,128]{1,0:T(8,128)(2,1)S(1)}, bf16[1024,128]{1,0:T(8,128)(2,1)S(1)}, u32[]{:S(2)}, u32[]{:S(2)}) collective-permute-start(bf16[1024,128]{1,0:T(8,128)(2,1)S(1)} %get-tuple-element.410), channel_id=1, source_target_pairs={{0,4},{4,8},{8,12},{12,16},{16,20},{20,24},{24,28},{28,0},{1,5},{5... | collective-permute-start | bytes 786440 | tf_op jit(solution)/shard_map/while/body/eval_jaxpr/ppermute | solution.py:15
  50.9 11.9 %collective-permute-start = (bf16[1024,128]{1,0:T(8,128)(2,1)S(1)}, bf16[1024,128]{1,0:T(8,128)(2,1)S(1)}, u32[]{:S(2)}, u32[]{:S(2)}) collective-permute-start(bf16[1024,128]{1,0:T(8,128)(2,1)S(1)} %get-tuple-element.409), channel_id=1, source_target_pairs={{0,4},{4,8},{8,12},{12,16},{16,20},{20,24},{24,28},{28,0},{1,5},{5... | collective-permute-start | bytes 786440 | tf_op jit(solution)/shard_map/while/body/eval_jaxpr/ppermute | solution.py:15
  51.0 14.9 %collective-permute-start.1 = (bf16[1024,128]{1,0:T(8,128)(2,1)S(1)}, bf16[1024,128]{1,0:T(8,128)(2,1)S(1)}, u32[]{:S(2)}, u32[]{:S(2)}) collective-permute-start(bf16[1024,128]{1,0:T(8,128)(2,1)S(1)} %get-tuple-element.410), channel_id=1, source_target_pairs={{0,4},{4,8},{8,12},{12,16},{16,20},{20,24},{24,28},{28,0},{1,5},{5... | collective-permute-start | bytes 786440 | tf_op jit(solution)/shard_map/while/body/eval_jaxpr/ppermute | solution.py:15
  66.0 11.3 %collective-permute-start = (bf16[1024,128]{1,0:T(8,128)(2,1)S(1)}, bf16[1024,128]{1,0:T(8,128)(2,1)S(1)}, u32[]{:S(2)}, u32[]{:S(2)}) collective-permute-start(bf16[1024,128]{1,0:T(8,128)(2,1)S(1)} %get-tuple-element.409), channel_id=1, source_target_pairs={{0,4},{4,8},{8,12},{12,16},{16,20},{20,24},{24,28},{28,0},{1,5},{5... | collective-permute-start | bytes 786440 | tf_op jit(solution)/shard_map/while/body/eval_jaxpr/ppermute | solution.py:15
  68.5 11.6 %collective-permute-start.1 = (bf16[1024,128]{1,0:T(8,128)(2,1)S(1)}, bf16[1024,128]{1,0:T(8,128)(2,1)S(1)}, u32[]{:S(2)}, u32[]{:S(2)}) collective-permute-start(bf16[1024,128]{1,0:T(8,128)(2,1)S(1)} %get-tuple-element.410), channel_id=1, source_target_pairs={{0,4},{4,8},{8,12},{12,16},{16,20},{20,24},{24,28},{28,0},{1,5},{5... | collective-permute-start | bytes 786440 | tf_op jit(solution)/shard_map/while/body/eval_jaxpr/ppermute | solution.py:15
  85.0 10.5 %collective-permute-start = (bf16[1024,128]{1,0:T(8,128)(2,1)S(1)}, bf16[1024,128]{1,0:T(8,128)(2,1)S(1)}, u32[]{:S(2)}, u32[]{:S(2)}) collective-permute-start(bf16[1024,128]{1,0:T(8,128)(2,1)S(1)} %get-tuple-element.409), channel_id=1, source_target_pairs={{0,4},{4,8},{8,12},{12,16},{16,20},{20,24},{24,28},{28,0},{1,5},{5... | collective-permute-start | bytes 786440 | tf_op jit(solution)/shard_map/while/body/eval_jaxpr/ppermute | solution.py:15
  85.1 13.1 %collective-permute-start.1 = (bf16[1024,128]{1,0:T(8,128)(2,1)S(1)}, bf16[1024,128]{1,0:T(8,128)(2,1)S(1)}, u32[]{:S(2)}, u32[]{:S(2)}) collective-permute-start(bf16[1024,128]{1,0:T(8,128)(2,1)S(1)} %get-tuple-element.410), channel_id=1, source_target_pairs={{0,4},{4,8},{8,12},{12,16},{16,20},{20,24},{24,28},{28,0},{1,5},{5... | collective-permute-start | bytes 786440 | tf_op jit(solution)/shard_map/while/body/eval_jaxpr/ppermute | solution.py:15
  103.3 9.6 %collective-permute-start = (bf16[1024,128]{1,0:T(8,128)(2,1)S(1)}, bf16[1024,128]{1,0:T(8,128)(2,1)S(1)}, u32[]{:S(2)}, u32[]{:S(2)}) collective-permute-start(bf16[1024,128]{1,0:T(8,128)(2,1)S(1)} %get-tuple-element.409), channel_id=1, source_target_pairs={{0,4},{4,8},{8,12},{12,16},{16,20},{20,24},{24,28},{28,0},{1,5},{5... | collective-permute-start | bytes 786440 | tf_op jit(solution)/shard_map/while/body/eval_jaxpr/ppermute | solution.py:15
  103.3 12.3 %collective-permute-start.1 = (bf16[1024,128]{1,0:T(8,128)(2,1)S(1)}, bf16[1024,128]{1,0:T(8,128)(2,1)S(1)}, u32[]{:S(2)}, u32[]{:S(2)}) collective-permute-start(bf16[1024,128]{1,0:T(8,128)(2,1)S(1)} %get-tuple-element.410), channel_id=1, source_target_pairs={{0,4},{4,8},{8,12},{12,16},{16,20},{20,24},{24,28},{28,0},{1,5},{5... | collective-permute-start | bytes 786440 | tf_op jit(solution)/shard_map/while/body/eval_jaxpr/ppermute | solution.py:15
  120.6 9.1 %collective-permute-start = (bf16[1024,128]{1,0:T(8,128)(2,1)S(1)}, bf16[1024,128]{1,0:T(8,128)(2,1)S(1)}, u32[]{:S(2)}, u32[]{:S(2)}) collective-permute-start(bf16[1024,128]{1,0:T(8,128)(2,1)S(1)} %get-tuple-element.409), channel_id=1, source_target_pairs={{0,4},{4,8},{8,12},{12,16},{16,20},{20,24},{24,28},{28,0},{1,5},{5... | collective-permute-start | bytes 786440 | tf_op jit(solution)/shard_map/while/body/eval_jaxpr/ppermute | solution.py:15
  120.7 11.9 %collective-permute-start.1 = (bf16[1024,128]{1,0:T(8,128)(2,1)S(1)}, bf16[1024,128]{1,0:T(8,128)(2,1)S(1)}, u32[]{:S(2)}, u32[]{:S(2)}) collective-permute-start(bf16[1024,128]{1,0:T(8,128)(2,1)S(1)} %get-tuple-element.410), channel_id=1, source_target_pairs={{0,4},{4,8},{8,12},{12,16},{16,20},{20,24},{24,28},{28,0},{1,5},{5... | collective-permute-start | bytes 786440 | tf_op jit(solution)/shard_map/while/body/eval_jaxpr/ppermute | solution.py:15
where the time goes:
time: 136 us; the launch traced here: 134 us
  waiting for transfers between devices  78.3 us (58%)
  matrix products  19.2 us (14%)
  starting transfers between devices  11.4 us (8%)
  other arithmetic  9.07 us (7%)
  loops' own time  8.8 us (6%)
  local copies, waits for them, and re-layouts  7.03 us (5%)
    ppermute x14, waiting for transfers between devices, shifted(): lax.ppermute(array, axis, [(i, (i + by) % count) for i in range(count)])  78.3 us
    ppermute x14, starting transfers between devices, shifted(): lax.ppermute(array, axis, [(i, (i + by) % count) for i in range(count)])  11.4 us
    dot_general x5, matrix products, fresh_partial(): jnp.einsum('hqk,kd->hqd', weights.astype(jnp.bfloat16), value_block, pref...  11.3 us
    another operation x1, loops' own time, body(): lax.fori_loop(1, devices, cycle_step, (key_rows, value_rows, carried))  8.76 us
    dot_general x5, matrix products, score_tile(): jnp.einsum('qhd,kd->hqk', query_heads, key_block, preferred_element_type=...  7.88 us
    reduce_sum x5, other arithmetic, fresh_partial(): row_total = jnp.sum(weights, axis=2)  7.49 us
    dynamic_slice x7, local copies, waits for them, and re-layouts, cycle_step(): block_order[source] < my_block  4.27 us
  transfers between devices with their start and end apart: 14, of which 14 were waited for; matrix products, arithmetic and copies ran while one was open for 3% of the time, Pallas kernels for 0%

commit v1 on v0

v1 whole, which is shorter than its diff:
```python
import functools

import jax
import jax.numpy as jnp
from jax import lax
from jax.experimental import pallas as pl
from jax.experimental.pallas import tpu as pltpu
from jax.sharding import PartitionSpec as P

HD = 128
QH = 2
CHUNKS = 4
TILE = 256
SCALE2 = 168.0 ** (-0.5) * 1.4426950408889634
LOW = -1e30


def ring_place(index, count):
    side = lax.rem(index, 2)
    level = lax.div(index, 2)
    return level * (1 - side) + (count - 1 - level) * side


def ring_index(place, count):
    side = lax.div(place, count // 2)
    level = place * (1 - side) + (count - 1 - place) * side
    return level * 2 + side


def lanes(column, width):
    return jnp.concatenate([column] * (width // HD), axis=1)


def dot_t(a, b):
    return lax.dot_general(a, b, (((1,), (1,)), ((), ())), preferred_element_type=jnp.float32)


def lane_sum(weights):
    total = weights[:, :HD]
    for start in range(HD, weights.shape[1], HD):
        total = total + weights[:, start : start + HD]
    return total


def kernel(
    count, order_ref, q_ref, k_ref, v_ref, out_ref,
    left_k, left_v, right_k, right_v, acc, peak, total,
    to_right, to_left, from_left, from_right,
):
    me = lax.axis_index("ctx")
    rows = q_ref.shape[0]
    piece = rows // CHUNKS
    steps = CHUNKS * (count - 1) // 2
    place = ring_place(me, count)
    right = ring_index(lax.rem(place + 1, count), count)
    left = ring_index(lax.rem(place + count - 1, count), count)

    barrier = pltpu.get_barrier_semaphore()
    for neighbour in (left, right):
        pl.semaphore_signal(barrier, inc=1, device_id={"ctx": neighbour}, device_id_type=pl.DeviceIdType.MESH)
    pl.semaphore_wait(barrier, 2)

    def copies(j, to_the_right, k_src, v_src):
        k_dst, v_dst = (left_k, left_v) if to_the_right else (right_k, right_v)
        send, recv = (to_right, from_left) if to_the_right else (to_left, from_right)
        target = right if to_the_right else left
        return [
            pltpu.make_async_remote_copy(
                src_ref=src, dst_ref=dst.at[j], send_sem=send.at[j, which], recv_sem=recv.at[j, which],
                device_id={"ctx": target}, device_id_type=pl.DeviceIdType.MESH,
            )
            for which, (src, dst) in enumerate(((k_src, k_dst), (v_src, v_dst)))
        ]

    def own(j, to_the_right):
        at = (j if to_the_right else (j + CHUNKS // 2) % CHUNKS) * piece
        return k_ref.at[pl.ds(at, piece)], v_ref.at[pl.ds(at, piece)]

    for j in range(CHUNKS):
        for way in (True, False):
            for copy in copies(j, way, *own(j, way)):
                copy.start()

    for head in range(QH):
        cols = slice(head * HD, (head + 1) * HD)
        for tile in range(rows // TILE):
            here = slice(tile * TILE, (tile + 1) * TILE)
            width = (tile + 1) * TILE
            scores = dot_t(q_ref[here, cols], k_ref[:width, :])
            row_ids = lax.broadcasted_iota(jnp.int32, (TILE, width), 0) + tile * TILE
            column_ids = lax.broadcasted_iota(jnp.int32, (TILE, width), 1)
            scores = jnp.where(column_ids <= row_ids, scores, LOW)
            top = jnp.broadcast_to(jnp.max(scores, axis=1, keepdims=True), (TILE, HD))
            weights = jnp.exp2((scores - lanes(top, width)) * SCALE2)
            total[head, here, :] = lane_sum(weights)
            acc[head, here, :] = jnp.dot(
                weights.astype(jnp.bfloat16), v_ref[:width, :], preferred_element_type=jnp.float32
            )
            peak[head, here, :] = top

    mine = order_ref[me]

    def absorb(j, carry):
        for way in (True, False):
            for copy in copies(j, way, *own(0, way)):
                copy.wait_recv()

        @pl.when(j + CHUNKS < steps)
        def _():
            for way, k_src, v_src in ((True, left_k, left_v), (False, right_k, right_v)):
                for copy in copies(j + CHUNKS, way, k_src.at[j], v_src.at[j]):
                    copy.start()

        far = 1 + lax.div(j, CHUNKS)
        see_left = order_ref[ring_index(lax.rem(place + count - far, count), count)] < mine
        see_right = order_ref[ring_index(lax.rem(place + far, count), count)] < mine

        def tile_step(tile, carry):
            here = pl.ds(pl.multiple_of(tile * TILE, TILE), TILE)
            for head in range(QH):
                cols = slice(head * HD, (head + 1) * HD)
                q = q_ref[here, cols]
                first = dot_t(q, left_k[j])
                second = dot_t(q, right_k[j])
                old = peak[head, here, :]
                top_first = jnp.where(see_left, jnp.max(first, axis=1, keepdims=True), LOW)
                top_second = jnp.where(see_right, jnp.max(second, axis=1, keepdims=True), LOW)
                top = jnp.maximum(old, jnp.maximum(top_first, top_second))
                keep = jnp.exp2((old - top) * SCALE2)
                shift_first = jnp.where(see_left, top, -LOW)
                shift_second = jnp.where(see_right, top, -LOW)
                w_first = jnp.exp2((first - lanes(shift_first, piece)) * SCALE2)
                w_second = jnp.exp2((second - lanes(shift_second, piece)) * SCALE2)
                peak[head, here, :] = top
                total[head, here, :] = total[head, here, :] * keep + (lane_sum(w_first) + lane_sum(w_second))
                acc[head, here, :] = acc[head, here, :] * keep + (
                    jnp.dot(w_first.astype(jnp.bfloat16), left_v[j], preferred_element_type=jnp.float32)
                    + jnp.dot(w_second.astype(jnp.bfloat16), right_v[j], preferred_element_type=jnp.float32)
                )
            return carry

        return lax.fori_loop(0, rows // TILE, tile_step, carry)

    lax.fori_loop(0, steps, absorb, 0)

    for head in range(QH):
        cols = slice(head * HD, (head + 1) * HD)
        whole = jnp.sum(total[head], axis=1, keepdims=True)
        out_ref[:, cols] = (acc[head] / whole).astype(out_ref.dtype)

    def drain(j, carry):
        for way in (True, False):
            for copy in copies(j, way, *own(0, way)):
                copy.wait_send()
        return carry

    lax.fori_loop(0, steps, drain, 0)


def solution(mesh):
    count = mesh.shape["ctx"]
    steps = CHUNKS * (count - 1) // 2

    def body(queries, key_rows, value_rows, block_order):
        rows = queries.shape[0]
        piece = rows // CHUNKS
        slots = pltpu.VMEM((steps, piece, HD), jnp.bfloat16)
        stats = pltpu.VMEM((QH, rows, HD), jnp.float32)
        sems = pltpu.SemaphoreType.DMA((steps, 2))
        vmem = pl.BlockSpec(memory_space=pltpu.VMEM)
        return pl.pallas_call(
            functools.partial(kernel, count),
            out_shape=jax.ShapeDtypeStruct(queries.shape, queries.dtype),
            in_specs=[pl.BlockSpec(memory_space=pltpu.SMEM), vmem, vmem, vmem],
            out_specs=vmem,
            scratch_shapes=[slots] * 4 + [stats] * 3 + [sems] * 4,
            compiler_params=pltpu.CompilerParams(
                collective_id=0, has_side_effects=True, vmem_limit_bytes=48 * 1024 * 1024
            ),
        )(block_order, queries, key_rows, value_rows)

    in_specs = (P("ctx", "head"), P("ctx", "head"), P("ctx", "head"), P())
    return jax.shard_map(body, mesh=mesh, in_specs=in_specs, out_specs=P("ctx", "head"), check_vma=False)
```

time: 136 us -> 62.4 us (0.46); the launches traced: 134 us -> 62.2 us
  waiting for transfers between devices: 78.3 us -> 0 us
  Pallas kernels: 0 us -> 57.8 us
  matrix products: 19.2 us -> 0 us
  starting transfers between devices: 11.4 us -> 0 us
  other arithmetic: 9.07 us -> 0 us
  loops' own time: 8.8 us -> 0 us
  local copies, waits for them, and re-layouts: 7.03 us -> 4.39 us
    ppermute x14 -> x0, waiting for transfers between devices: 78.3 us -> none  [shifted(): lax.ppermute(array, axis, [(i, (i + by) % count) for i in range(count)])]
    pallas_call x0 -> x1, Pallas kernels: none -> 57.8 us  [body(): pl.pallas_call(functools.partial(kernel, count), out_shape=jax.ShapeDtype...]
    dot_general x10 -> x0, matrix products: 19.2 us -> none  [the longest x5 11.3 us: fresh_partial(): jnp.einsum('hqk,kd->hqd', weights.astype(jnp.bfloat16), value_block, pref...]
    ppermute x14 -> x0, starting transfers between devices: 11.4 us -> none  [shifted(): lax.ppermute(array, axis, [(i, (i + by) % count) for i in range(count)])]
    another operation x8 -> x0, loops' own time: 8.8 us -> none  [the longest x1 8.76 us: body(): lax.fori_loop(1, devices, cycle_step, (key_rows, value_rows, carried))]
    reduce_sum x5 -> x0, other arithmetic: 7.49 us -> none  [fresh_partial(): row_total = jnp.sum(weights, axis=2)]
    dynamic_slice x8 -> x0, local copies, waits for them, and re-layouts: 4.85 us -> none  [the longest x7 4.27 us: cycle_step(): block_order[source] < my_block]
    unnamed x6 -> x9, local copies, waits for them, and re-layouts: 1.91 us -> 4.39 us
  transfers between devices with their start and end apart: 14 -> 0, of which waited for: 14 -> 0; matrix products, arithmetic and copies ran while one was open for 3% -> 0% of each run, Pallas kernels for 0% -> 0%
where the time goes in v1:
time: 62.4 us; the launch traced here: 62.2 us
  Pallas kernels  57.8 us (93%)
  local copies, waits for them, and re-layouts  4.39 us (7%)
    pallas_call x1, Pallas kernels, body(): pl.pallas_call(functools.partial(kernel, count), out_shape=jax.ShapeDtype...  57.8 us
    unnamed x9, local copies, waits for them, and re-layouts  4.39 us

profile of v1, /device:TPU:0, one launch (start us, length us, event | category | flops | bytes accessed | tf_op | source)
XLA Modules:
  0.0 62.2 jit_solution(2959226280779613463)
XLA Ops:
  0.0 0.0 copy-start
  0.0 1.0 %copy-done = bf16[1024,256]{1,0:T(8,128)(2,1)S(1)} copy-done((bf16[1024,256]{1,0:T(8,128)(2,1)S(1)}, bf16[1024,256]{1,0:T(8,128)(2,1)}, u32[]{:S(2)}) %copy-start) | copy-done | bytes 524312
  1.0 0.0 copy-start.1
  1.0 0.9 %copy-done.1 = bf16[1024,128]{1,0:T(8,128)(2,1)S(1)} copy-done((bf16[1024,128]{1,0:T(8,128)(2,1)S(1)}, bf16[1024,128]{1,0:T(8,128)(2,1)}, u32[]{:S(2)}) %copy-start.1) | copy-done | bytes 262168
  2.0 0.0 copy-start.2
  2.0 0.9 %copy-done.2 = bf16[1024,128]{1,0:T(8,128)(2,1)S(1)} copy-done((bf16[1024,128]{1,0:T(8,128)(2,1)S(1)}, bf16[1024,128]{1,0:T(8,128)(2,1)}, u32[]{:S(2)}) %copy-start.2) | copy-done | bytes 262168
  2.9 0.0 copy-start.3
  2.9 0.7 %copy-done.3 = s32[8]{0:T(128)S(1)} copy-done((s32[8]{0:T(128)S(1)}, s32[8]{0:T(128)}, u32[]{:S(2)}) %copy-start.3) | copy-done | bytes 56
  3.6 57.8 %shard_map.46 = bf16[1024,256]{1,0:T(8,128)(2,1)S(1)} custom-call(s32[8]{0:T(128)S(1)} %copy-done.3, bf16[1024,256]{1,0:T(8,128)(2,1)S(1)} %copy-done, bf16[1024,128]{1,0:T(8,128)(2,1)S(1)} %copy-done.1, bf16[1024,128]{1,0:T(8,128)(2,1)S(1)} %copy-done.2), custom_call_target="tpu_custom_call" | custom-call | tf_op jit(solution)/shard_map/pallas_call | solution.py:171
  61.4 0.8 %copy.6 = bf16[1024,256]{1,0:T(8,128)(2,1)} copy(bf16[1024,256]{1,0:T(8,128)(2,1)S(1)} %shard_map.46) | data formatting | bytes 1048576
Async XLA Ops:
  0.0 1.0 %copy-start = (bf16[1024,256]{1,0:T(8,128)(2,1)S(1)}, bf16[1024,256]{1,0:T(8,128)(2,1)}, u32[]{:S(2)}) copy-start(bf16[1024,256]{1,0:T(8,128)(2,1)} %q_ref.1) | copy-start | bytes 1572868
  1.0 0.9 %copy-start.1 = (bf16[1024,128]{1,0:T(8,128)(2,1)S(1)}, bf16[1024,128]{1,0:T(8,128)(2,1)}, u32[]{:S(2)}) copy-start(bf16[1024,128]{1,0:T(8,128)(2,1)} %k_ref.1) | copy-start | bytes 786436
  2.0 0.9 %copy-start.2 = (bf16[1024,128]{1,0:T(8,128)(2,1)S(1)}, bf16[1024,128]{1,0:T(8,128)(2,1)}, u32[]{:S(2)}) copy-start(bf16[1024,128]{1,0:T(8,128)(2,1)} %v_ref.1) | copy-start | bytes 786436
  2.9 0.7 %copy-start.3 = (s32[8]{0:T(128)S(1)}, s32[8]{0:T(128)}, u32[]{:S(2)}) copy-start(s32[8]{0:T(128)} %order_ref.1) | copy-start | bytes 100

commit v2 on v1

--- a/solution.py
+++ b/solution.py
@@ -10,7 +10,8 @@
 HD = 128
 QH = 2
 CHUNKS = 4
-TILE = 256
+TILE = 1024
+EDGE = 256
 SCALE2 = 168.0 ** (-0.5) * 1.4426950408889634
 LOW = -1e30
 
@@ -43,12 +44,14 @@
 
 
 def kernel(
-    count, order_ref, q_ref, k_ref, v_ref, out_ref,
+    count, order_hbm, q_hbm, k_hbm, v_hbm, out_ref,
+    order_ref, q_ref, k_ref, v_ref,
     left_k, left_v, right_k, right_v, acc, peak, total,
-    to_right, to_left, from_left, from_right,
+    to_right, to_left, from_left, from_right, loaded,
 ):
     me = lax.axis_index("ctx")
     rows = q_ref.shape[0]
+    band = min(TILE, rows)
     piece = rows // CHUNKS
     steps = CHUNKS * (count - 1) // 2
     place = ring_place(me, count)
@@ -58,6 +61,12 @@
     barrier = pltpu.get_barrier_semaphore()
     for neighbour in (left, right):
         pl.semaphore_signal(barrier, inc=1, device_id={"ctx": neighbour}, device_id_type=pl.DeviceIdType.MESH)
+    loads = [
+        pltpu.make_async_copy(src, dst, loaded.at[which])
+        for which, (src, dst) in enumerate(((order_hbm, order_ref), (k_hbm, k_ref), (q_hbm, q_ref), (v_hbm, v_ref)))
+    ]
+    for load in loads:
+        load.start()
     pl.semaphore_wait(barrier, 2)
 
     def copies(j, to_the_right, k_src, v_src):
@@ -74,23 +83,26 @@
 
     def own(j, to_the_right):
         at = (j if to_the_right else (j + CHUNKS // 2) % CHUNKS) * piece
-        return k_ref.at[pl.ds(at, piece)], v_ref.at[pl.ds(at, piece)]
+        return k_hbm.at[pl.ds(at, piece)], v_hbm.at[pl.ds(at, piece)]
 
     for j in range(CHUNKS):
         for way in (True, False):
             for copy in copies(j, way, *own(j, way)):
                 copy.start()
 
+    for load in loads:
+        load.wait()
+
     for head in range(QH):
         cols = slice(head * HD, (head + 1) * HD)
-        for tile in range(rows // TILE):
-            here = slice(tile * TILE, (tile + 1) * TILE)
-            width = (tile + 1) * TILE
+        for tile in range(rows // EDGE):
+            here = slice(tile * EDGE, (tile + 1) * EDGE)
+            width = (tile + 1) * EDGE
             scores = dot_t(q_ref[here, cols], k_ref[:width, :])
-            row_ids = lax.broadcasted_iota(jnp.int32, (TILE, width), 0) + tile * TILE
-            column_ids = lax.broadcasted_iota(jnp.int32, (TILE, width), 1)
+            row_ids = lax.broadcasted_iota(jnp.int32, (EDGE, width), 0) + tile * EDGE
+            column_ids = lax.broadcasted_iota(jnp.int32, (EDGE, width), 1)
             scores = jnp.where(column_ids <= row_ids, scores, LOW)
-            top = jnp.broadcast_to(jnp.max(scores, axis=1, keepdims=True), (TILE, HD))
+            top = jnp.broadcast_to(jnp.max(scores, axis=1, keepdims=True), (EDGE, HD))
             weights = jnp.exp2((scores - lanes(top, width)) * SCALE2)
             total[head, here, :] = lane_sum(weights)
             acc[head, here, :] = jnp.dot(
@@ -116,7 +128,7 @@
         see_right = order_ref[ring_index(lax.rem(place + far, count), count)] < mine
 
         def tile_step(tile, carry):
-            here = pl.ds(pl.multiple_of(tile * TILE, TILE), TILE)
+            here = pl.ds(pl.multiple_of(tile * band, band), band)
             for head in range(QH):
                 cols = slice(head * HD, (head + 1) * HD)
                 q = q_ref[here, cols]
@@ -139,14 +151,14 @@
                 )
             return carry
 
-        return lax.fori_loop(0, rows // TILE, tile_step, carry)
+        return lax.fori_loop(0, rows // band, tile_step, carry)
 
     lax.fori_loop(0, steps, absorb, 0)
 
     for head in range(QH):
         cols = slice(head * HD, (head + 1) * HD)
-        whole = jnp.sum(total[head], axis=1, keepdims=True)
-        out_ref[:, cols] = (acc[head] / whole).astype(out_ref.dtype)
+        scale = 1.0 / jnp.sum(total[head], axis=1, keepdims=True)
+        out_ref[:, cols] = (acc[head] * scale).astype(out_ref.dtype)
 
     def drain(j, carry):
         for way in (True, False):
@@ -167,13 +179,15 @@
         slots = pltpu.VMEM((steps, piece, HD), jnp.bfloat16)
         stats = pltpu.VMEM((QH, rows, HD), jnp.float32)
         sems = pltpu.SemaphoreType.DMA((steps, 2))
-        vmem = pl.BlockSpec(memory_space=pltpu.VMEM)
+        local = [pltpu.SMEM(block_order.shape, block_order.dtype)] + [
+            pltpu.VMEM(array.shape, array.dtype) for array in (queries, key_rows, value_rows)
+        ]
         return pl.pallas_call(
             functools.partial(kernel, count),
             out_shape=jax.ShapeDtypeStruct(queries.shape, queries.dtype),
-            in_specs=[pl.BlockSpec(memory_space=pltpu.SMEM), vmem, vmem, vmem],
-            out_specs=vmem,
-            scratch_shapes=[slots] * 4 + [stats] * 3 + [sems] * 4,
+            in_specs=[pl.BlockSpec(memory_space=pltpu.HBM)] * 4,
+            out_specs=pl.BlockSpec(memory_space=pltpu.VMEM),
+            scratch_shapes=local + [slots] * 4 + [stats] * 3 + [sems] * 4 + [pltpu.SemaphoreType.DMA((4,))],
             compiler_params=pltpu.CompilerParams(
                 collective_id=0, has_side_effects=True, vmem_limit_bytes=48 * 1024 * 1024
             ),

time: 62.4 us -> 52.5 us (0.84)
  Pallas kernels: 57.8 us -> 47.9 us
    pallas_call x1, Pallas kernels: 57.8 us -> 47.9 us  [body(): pl.pallas_call(functools.partial(kernel, count), out_shape=jax.ShapeDtype...]
where the time goes in v2:
time: 52.5 us; the launch traced here: 52.3 us
  Pallas kernels  47.9 us (91%)
  local copies, waits for them, and re-layouts  4.39 us (8%)
    pallas_call x1, Pallas kernels, body(): pl.pallas_call(functools.partial(kernel, count), out_shape=jax.ShapeDtype...  47.9 us
    unnamed x9, local copies, waits for them, and re-layouts  4.39 us

profile of v2, /device:TPU:0, one launch (start us, length us, event | category | flops | bytes accessed | tf_op | source)
XLA Modules:
  0.0 52.3 jit_solution(1992391068812500172)
XLA Ops:
  0.0 0.0 copy-start
  0.0 1.0 %copy-done = bf16[1024,256]{1,0:T(8,128)(2,1)S(1)} copy-done((bf16[1024,256]{1,0:T(8,128)(2,1)S(1)}, bf16[1024,256]{1,0:T(8,128)(2,1)}, u32[]{:S(2)}) %copy-start) | copy-done | bytes 524312
  1.0 0.0 copy-start.1
  1.0 0.9 %copy-done.1 = bf16[1024,128]{1,0:T(8,128)(2,1)S(1)} copy-done((bf16[1024,128]{1,0:T(8,128)(2,1)S(1)}, bf16[1024,128]{1,0:T(8,128)(2,1)}, u32[]{:S(2)}) %copy-start.1) | copy-done | bytes 262168
  2.0 0.0 copy-start.2
  2.0 0.9 %copy-done.2 = bf16[1024,128]{1,0:T(8,128)(2,1)S(1)} copy-done((bf16[1024,128]{1,0:T(8,128)(2,1)S(1)}, bf16[1024,128]{1,0:T(8,128)(2,1)}, u32[]{:S(2)}) %copy-start.2) | copy-done | bytes 262168
  2.9 0.0 copy-start.3
  2.9 0.7 %copy-done.3 = s32[8]{0:T(128)S(1)} copy-done((s32[8]{0:T(128)S(1)}, s32[8]{0:T(128)}, u32[]{:S(2)}) %copy-start.3) | copy-done | bytes 56
  3.6 47.9 %shard_map.46 = bf16[1024,256]{1,0:T(8,128)(2,1)S(1)} custom-call(s32[8]{0:T(128)S(1)} %copy-done.3, bf16[1024,256]{1,0:T(8,128)(2,1)S(1)} %copy-done, bf16[1024,128]{1,0:T(8,128)(2,1)S(1)} %copy-done.1, bf16[1024,128]{1,0:T(8,128)(2,1)S(1)} %copy-done.2), custom_call_target="tpu_custom_call" | custom-call | tf_op jit(solution)/shard_map/pallas_call | solution.py:185
  51.5 0.8 %copy.6 = bf16[1024,256]{1,0:T(8,128)(2,1)} copy(bf16[1024,256]{1,0:T(8,128)(2,1)S(1)} %shard_map.46) | data formatting | bytes 1048576
Async XLA Ops:
  0.0 1.0 %copy-start = (bf16[1024,256]{1,0:T(8,128)(2,1)S(1)}, bf16[1024,256]{1,0:T(8,128)(2,1)}, u32[]{:S(2)}) copy-start(bf16[1024,256]{1,0:T(8,128)(2,1)} %q_hbm.1) | copy-start | bytes 1572868
  1.0 0.9 %copy-start.1 = (bf16[1024,128]{1,0:T(8,128)(2,1)S(1)}, bf16[1024,128]{1,0:T(8,128)(2,1)}, u32[]{:S(2)}) copy-start(bf16[1024,128]{1,0:T(8,128)(2,1)} %k_hbm.1) | copy-start | bytes 786436
  2.0 0.9 %copy-start.2 = (bf16[1024,128]{1,0:T(8,128)(2,1)S(1)}, bf16[1024,128]{1,0:T(8,128)(2,1)}, u32[]{:S(2)}) copy-start(bf16[1024,128]{1,0:T(8,128)(2,1)} %v_hbm.1) | copy-start | bytes 786436
  2.9 0.7 %copy-start.3 = (s32[8]{0:T(128)S(1)}, s32[8]{0:T(128)}, u32[]{:S(2)}) copy-start(s32[8]{0:T(128)} %order_hbm.1) | copy-start | bytes 100

commit v3 on v2

v3 whole, which is shorter than its diff:
```python
import functools

import jax
import jax.numpy as jnp
from jax import lax
from jax.experimental import pallas as pl
from jax.experimental.pallas import tpu as pltpu
from jax.sharding import PartitionSpec as P

HD = 128
QH = 2
CHUNKS = 4
TILE = 1024
SCALE2 = 168.0 ** (-0.5) * 1.4426950408889634
LOW = -1e30


def ring_place(index, count):
    side = lax.rem(index, 2)
    level = lax.div(index, 2)
    return level * (1 - side) + (count - 1 - level) * side


def ring_index(place, count):
    side = lax.div(place, count // 2)
    level = place * (1 - side) + (count - 1 - place) * side
    return level * 2 + side


def lanes(column, width):
    return jnp.concatenate([column] * (width // HD), axis=1)


def dot_t(a, b):
    return lax.dot_general(a, b, (((1,), (1,)), ((), ())), preferred_element_type=jnp.float32)


def lane_sum(weights):
    total = weights[:, :HD]
    for start in range(HD, weights.shape[1], HD):
        total = total + weights[:, start : start + HD]
    return total


def kernel(
    count, order_hbm, q_hbm, k_hbm, v_hbm, out_ref,
    order_ref, q_ref, kv_ref, from_left, from_right, acc, peak, total,
    to_right_sem, to_left_sem, from_left_sem, from_right_sem, loaded,
):
    me = lax.axis_index("ctx")
    rows = q_ref.shape[0]
    band = min(TILE, rows)
    piece = rows // CHUNKS
    steps = CHUNKS * (count - 1) // 2
    place = ring_place(me, count)
    right = ring_index(lax.rem(place + 1, count), count)
    left = ring_index(lax.rem(place + count - 1, count), count)

    barrier = pltpu.get_barrier_semaphore()
    for neighbour in (left, right):
        pl.semaphore_signal(barrier, inc=1, device_id={"ctx": neighbour}, device_id_type=pl.DeviceIdType.MESH)
    def chunked(src, which):
        return [(src.at[pl.ds(c * piece, piece)], kv_ref.at[c, which]) for c in range(CHUNKS)]

    loads = [
        pltpu.make_async_copy(src, dst, loaded.at[which])
        for which, (src, dst) in enumerate(
            chunked(k_hbm, 0) + chunked(v_hbm, 1) + [(q_hbm, q_ref), (order_hbm, order_ref)]
        )
    ]
    for load in loads:
        load.start()
    for load in loads[:-2]:
        load.wait()
    pl.semaphore_wait(barrier, 2)

    def copy(j, rightward, src, slot):
        dst, send, recv, target = (
            (from_left, to_right_sem, from_left_sem, right)
            if rightward
            else (from_right, to_left_sem, from_right_sem, left)
        )
        return pltpu.make_async_remote_copy(
            src_ref=src.at[slot], dst_ref=dst.at[j], send_sem=send.at[j], recv_sem=recv.at[j],
            device_id={"ctx": target}, device_id_type=pl.DeviceIdType.MESH,
        )

    for j in range(CHUNKS):
        copy(j, True, kv_ref, j).start()
        copy(j, False, kv_ref, (j + CHUNKS // 2) % CHUNKS).start()
    for load in loads[-2:]:
        load.wait()

    for head in range(QH):
        cols = slice(head * HD, (head + 1) * HD)
        for tile in range(CHUNKS):
            here = slice(tile * piece, (tile + 1) * piece)
            width = (tile + 1) * piece
            scores = dot_t(q_ref[here, cols], kv_ref[: tile + 1, 0].reshape(width, HD))
            row_ids = lax.broadcasted_iota(jnp.int32, (piece, width), 0) + tile * piece
            column_ids = lax.broadcasted_iota(jnp.int32, (piece, width), 1)
            scores = jnp.where(column_ids <= row_ids, scores, LOW)
            top = jnp.broadcast_to(jnp.max(scores, axis=1, keepdims=True), (piece, HD))
            weights = jnp.exp2((scores - lanes(top, width)) * SCALE2)
            total[head, here, :] = lane_sum(weights)
            acc[head, here, :] = jnp.dot(
                weights.astype(jnp.bfloat16), kv_ref[: tile + 1, 1].reshape(width, HD), preferred_element_type=jnp.float32
            )
            peak[head, here, :] = top

    mine = order_ref[me]

    def arrive(j):
        copy(j, True, kv_ref, 0).wait_recv()
        copy(j, False, kv_ref, 0).wait_recv()

    def absorb(j, last):
        far = 1 + lax.div(j, CHUNKS)
        see_left = order_ref[ring_index(lax.rem(place + count - far, count), count)] < mine
        see_right = order_ref[ring_index(lax.rem(place + far, count), count)] < mine

        def tile_step(tile, carry):
            here = pl.ds(pl.multiple_of(tile * band, band), band)
            for head in range(QH):
                cols = slice(head * HD, (head + 1) * HD)
                q = q_ref[here, cols]
                first = dot_t(q, from_left[j, 0])
                second = dot_t(q, from_right[j, 0])
                old = peak[head, here, :]
                top_first = jnp.where(see_left, jnp.max(first, axis=1, keepdims=True), LOW)
                top_second = jnp.where(see_right, jnp.max(second, axis=1, keepdims=True), LOW)
                top = jnp.maximum(old, jnp.maximum(top_first, top_second))
                keep = jnp.exp2((old - top) * SCALE2)
                shift_first = jnp.where(see_left, top, -LOW)
                shift_second = jnp.where(see_right, top, -LOW)
                w_first = jnp.exp2((first - lanes(shift_first, piece)) * SCALE2)
                w_second = jnp.exp2((second - lanes(shift_second, piece)) * SCALE2)
                new_total = total[head, here, :] * keep + (lane_sum(w_first) + lane_sum(w_second))
                new_acc = acc[head, here, :] * keep + (
                    jnp.dot(w_first.astype(jnp.bfloat16), from_left[j, 1], preferred_element_type=jnp.float32)
                    + jnp.dot(w_second.astype(jnp.bfloat16), from_right[j, 1], preferred_element_type=jnp.float32)
                )
                if last:
                    inverse = 1.0 / jnp.sum(new_total, axis=1, keepdims=True)
                    out_ref[here, cols] = (new_acc * inverse).astype(out_ref.dtype)
                else:
                    peak[head, here, :] = top
                    total[head, here, :] = new_total
                    acc[head, here, :] = new_acc
            return carry

        lax.fori_loop(0, rows // band, tile_step, 0)

    def advance(j, carry):
        arrive(j)

        @pl.when(j + CHUNKS < steps)
        def _():
            copy(j + CHUNKS, True, from_left, j).start()
            copy(j + CHUNKS, False, from_right, j).start()

        absorb(j, False)
        return carry

    lax.fori_loop(0, steps - 1, advance, 0)
    arrive(steps - 1)
    absorb(steps - 1, True)

    def drain(j, carry):
        copy(j, True, kv_ref, 0).wait_send()
        copy(j, False, kv_ref, 0).wait_send()
        return carry

    lax.fori_loop(0, steps, drain, 0)


def solution(mesh):
    count = mesh.shape["ctx"]
    steps = CHUNKS * (count - 1) // 2

    def body(queries, key_rows, value_rows, block_order):
        rows = queries.shape[0]
        piece = rows // CHUNKS
        slots = pltpu.VMEM((steps, 2, piece, HD), jnp.bfloat16)
        stats = pltpu.VMEM((QH, rows, HD), jnp.float32)
        sems = pltpu.SemaphoreType.DMA((steps,))
        local = [
            pltpu.SMEM(block_order.shape, block_order.dtype),
            pltpu.VMEM(queries.shape, queries.dtype),
            pltpu.VMEM((CHUNKS, 2, piece, HD), key_rows.dtype),
        ]
        return pl.pallas_call(
            functools.partial(kernel, count),
            out_shape=jax.ShapeDtypeStruct(queries.shape, queries.dtype),
            in_specs=[pl.BlockSpec(memory_space=pl.ANY)] * 4,
            out_specs=pl.BlockSpec(memory_space=pltpu.VMEM),
            scratch_shapes=local + [slots] * 2 + [stats] * 3 + [sems] * 4 + [pltpu.SemaphoreType.DMA((2 * CHUNKS + 2,))],
            compiler_params=pltpu.CompilerParams(
                collective_id=0, has_side_effects=True
            ),
        )(block_order, queries, key_rows, value_rows)

    in_specs = (P("ctx", "head"), P("ctx", "head"), P("ctx", "head"), P())
    return jax.shard_map(body, mesh=mesh, in_specs=in_specs, out_specs=P("ctx", "head"), check_vma=False)
```

time: 52.5 us -> 49.9 us (0.950)
  local copies, waits for them, and re-layouts: 4.39 us -> 1.87 us
    unnamed x9 -> x1, local copies, waits for them, and re-layouts: 4.39 us -> 1.87 us
where the time goes in v3:
time: 49.9 us; the launch traced here: 49.7 us
  Pallas kernels  47.8 us (96%)
  local copies, waits for them, and re-layouts  1.87 us (4%)
    pallas_call x1, Pallas kernels, body(): pl.pallas_call(functools.partial(kernel, count), out_shape=jax.ShapeDtype...  47.8 us
    unnamed x1, local copies, waits for them, and re-layouts  1.87 us

profile of v3, /device:TPU:0, one launch (start us, length us, event | category | flops | bytes accessed | tf_op | source)
XLA Modules:
  0.0 49.7 jit_solution(2437265135978205600)
XLA Ops:
  0.0 47.8 %shard_map.46 = bf16[1024,256]{1,0:T(8,128)(2,1)} custom-call(s32[8]{0:T(128)} %order_hbm.1, bf16[1024,256]{1,0:T(8,128)(2,1)} %q_hbm.1, bf16[1024,128]{1,0:T(8,128)(2,1)} %k_hbm.1, bf16[1024,128]{1,0:T(8,128)(2,1)} %v_hbm.1), custom_call_target="tpu_custom_call" | custom-call | tf_op jit(solution)/shard_map/pallas_call | solution.py:192
  47.9 1.9 %copy.6 = bf16[1024,256]{1,0:T(8,128)(2,1)} copy(bf16[1024,256]{1,0:T(8,128)(2,1)} %shard_map.46) | data formatting | bytes 1048576

commit v4 on v3

--- a/solution.py
+++ b/solution.py
@@ -192,13 +192,13 @@
         return pl.pallas_call(
             functools.partial(kernel, count),
             out_shape=jax.ShapeDtypeStruct(queries.shape, queries.dtype),
-            in_specs=[pl.BlockSpec(memory_space=pl.ANY)] * 4,
+            in_specs=[pl.BlockSpec(memory_space=pltpu.HBM)] * 4,
             out_specs=pl.BlockSpec(memory_space=pltpu.VMEM),
             scratch_shapes=local + [slots] * 2 + [stats] * 3 + [sems] * 4 + [pltpu.SemaphoreType.DMA((2 * CHUNKS + 2,))],
             compiler_params=pltpu.CompilerParams(
-                collective_id=0, has_side_effects=True
+                collective_id=0, has_side_effects=True, vmem_limit_bytes=48 * 1024 * 1024
             ),
-        )(block_order, queries, key_rows, value_rows)
+        )(*(pltpu.with_memory_space_constraint(x, pltpu.HBM) for x in (block_order, queries, key_rows, value_rows)))
 
     in_specs = (P("ctx", "head"), P("ctx", "head"), P("ctx", "head"), P())
     return jax.shard_map(body, mesh=mesh, in_specs=in_specs, out_specs=P("ctx", "head"), check_vma=False)

time: 49.9 us -> 48 us (0.962)
  local copies, waits for them, and re-layouts: 1.87 us -> 0.8 us
  Pallas kernels: 47.8 us -> 47.1 us
    unnamed x1, local copies, waits for them, and re-layouts: 1.87 us -> 0.8 us
    pallas_call x1, Pallas kernels: 47.8 us -> 47.1 us  [body(): pl.pallas_call(functools.partial(kernel, count), out_shape=jax.ShapeDtype...]
where the time goes in v4:
time: 48 us; the launch traced here: 47.9 us
  Pallas kernels  47.1 us (98%)
  local copies, waits for them, and re-layouts  0.8 us (2%)
    pallas_call x1, Pallas kernels, body(): pl.pallas_call(functools.partial(kernel, count), out_shape=jax.ShapeDtype...  47.1 us

profile of v4, /device:TPU:0, one launch (start us, length us, event | category | flops | bytes accessed | tf_op | source)
XLA Modules:
  0.0 47.9 jit_solution(12360624998881438629)
XLA Ops:
  0.0 47.1 %shard_map.46 = bf16[1024,256]{1,0:T(8,128)(2,1)S(1)} custom-call(s32[8]{0:T(128)} %order_hbm.1, bf16[1024,256]{1,0:T(8,128)(2,1)} %q_hbm.1, bf16[1024,128]{1,0:T(8,128)(2,1)} %k_hbm.1, bf16[1024,128]{1,0:T(8,128)(2,1)} %v_hbm.1), custom_call_target="tpu_custom_call" | custom-call | tf_op jit(solution)/shard_map/pallas_call | solution.py:192
  47.1 0.8 %copy.6 = bf16[1024,256]{1,0:T(8,128)(2,1)} copy(bf16[1024,256]{1,0:T(8,128)(2,1)S(1)} %shard_map.46) | data formatting | bytes 1048576
